TPU v7x, 32 devices: a whole 2x2x4 slice. The times are simulated.
32 devices in a mesh: groups: 2 (over y), slab: 4 (over z), batch: 2 (over x), chan: 2 (over core).
Axes of the slice: x: 2, y: 2, z: 4, core: 2. Of those that a mesh axis runs over, the one named last changes fastest.
Arguments:
- volume: bfloat16 [16, 8, 4, 8, 128], P(('groups', 'batch'), 'slab'), parts along dimension 0, may hold values from -6 to 6
- targets: float32 [16, 4], P(('groups', 'batch')), parts along dimension 0, may hold values from -1 to 1
- front_weight: bfloat16 [3, 3, 3, 128, 128], P(None, None, None, None, 'chan'), may hold values from -0.109375 to 0.109375
- stride_weight: bfloat16 [3, 3, 3, 128, 256], P(None, None, None, 'chan'), may hold values from -0.109375 to 0.109375
- hidden_weight: float32 [256, 128], P('chan'), may hold values from -0.375 to 0.375
- output_weight: float32 [128, 4], replicated, may hold values from -0.5 to 0.5
Outputs:
- grad_front: float32 [6, 3, 3, 128, 128], P('groups', None, None, None, 'chan'), parts along dimension 0
- grad_stride: float32 [6, 3, 3, 128, 256], P('groups', None, None, 'chan'), parts along dimension 0
- grad_hidden: float32 [512, 128], P(('groups', 'chan')), parts along dimension 0
- grad_output: float32 [256, 4], P('groups'), parts along dimension 0
- loss: float32 [2], P('groups'), parts along dimension 0
There are 2 independent parts, one for each index of `groups`. A program takes and returns all parts, laid end to end along the dimension named above; an argument that names none is the same for every part. Nothing has to cross between parts.
All inputs are finite; a program needn't handle non-finite values.
Results may differ from a plain program's by a relative error of at most 0.0052.
Values may be sent and summed in bfloat16 or wider, within the bound.
A program may use at most 64 MiB of HBM per device.

v0:
```python
import jax
import jax.numpy as jnp
from jax import lax
from jax.sharding import PartitionSpec as P


def with_halo(cells, sides, width):
    for axis, dim in sides:
        count = lax.axis_size(axis)
        ends = count - 1
        head = lax.slice_in_dim(cells, 0, width, axis=dim)
        tail = lax.slice_in_dim(cells, cells.shape[dim] - width, cells.shape[dim], axis=dim)
        cells = jnp.concatenate(
            [
                lax.ppermute(tail, axis, [(i, (i + 1) % count) for i in range(ends)]),
                cells,
                lax.ppermute(head, axis, [((i + 1) % count, i) for i in range(ends)]),
            ],
            axis=dim,
        )
    return cells


def swish_slope(preact):
    logistic = jax.nn.sigmoid(preact)
    return logistic * (1.0 + preact * (1.0 - logistic))


def tap_window(padded, tap_z, tap_x, tap_y, extent_z, extent_x, extent_y, stride):
    if stride == 1:
        return padded[
            :, tap_z : tap_z + extent_z, tap_x : tap_x + extent_x, tap_y : tap_y + extent_y, :
        ]
    leading = padded.shape[0]
    channels = padded.shape[-1]
    folded = padded.reshape(leading, extent_z + 1, 2, extent_x + 1, 2, extent_y + 1, 2, channels)
    return folded[
        :,
        tap_z // 2 : tap_z // 2 + extent_z,
        tap_z % 2,
        tap_x // 2 : tap_x // 2 + extent_x,
        tap_x % 2,
        tap_y // 2 : tap_y // 2 + extent_y,
        tap_y % 2,
        :,
    ]


def conv_apply(padded, weight, extent_z, extent_x, extent_y, stride):
    summed = None
    for tap_z in range(3):
        for tap_x in range(3):
            for tap_y in range(3):
                window = tap_window(
                    padded, tap_z, tap_x, tap_y, extent_z, extent_x, extent_y, stride
                )
                flat_tap = window.reshape(-1, window.shape[-1])
                contrib = jnp.dot(
                    flat_tap, weight[tap_z, tap_x, tap_y], preferred_element_type=jnp.float32
                )
                summed = contrib if summed is None else summed + contrib
    return summed.reshape(padded.shape[0], extent_z, extent_x, extent_y, weight.shape[-1])


def kernel_grad(padded, grad_out, extent_z, extent_x, extent_y, stride):
    flat_grad = grad_out.reshape(-1, grad_out.shape[-1])
    results = []
    for tap_z in range(3):
        for tap_x in range(3):
            for tap_y in range(3):
                window = tap_window(
                    padded, tap_z, tap_x, tap_y, extent_z, extent_x, extent_y, stride
                )
                flat_tap = window.reshape(-1, window.shape[-1])
                results.append(
                    lax.dot_general(
                        flat_tap,
                        flat_grad,
                        (((0,), (0,)), ((), ())),
                        preferred_element_type=jnp.float32,
                    )
                )
    return jnp.stack(results).reshape(3, 3, 3, padded.shape[-1], grad_out.shape[-1])


def input_grad(grad_out, weight, extent_z, extent_x, extent_y):
    leading = grad_out.shape[0]
    channels = weight.shape[3]
    flat_grad = grad_out.reshape(-1, grad_out.shape[-1])
    buckets = {}
    for tap_z in range(3):
        for tap_x in range(3):
            for tap_y in range(3):
                contrib = lax.dot_general(
                    flat_grad,
                    weight[tap_z, tap_x, tap_y],
                    (((1,), (1,)), ((), ())),
                    preferred_element_type=jnp.float32,
                )
                contrib = contrib.reshape(leading, extent_z, extent_x, extent_y, channels)
                placed = jnp.pad(
                    contrib,
                    (
                        (0, 0),
                        (tap_z // 2, 1 - tap_z // 2),
                        (tap_x // 2, 1 - tap_x // 2),
                        (tap_y // 2, 1 - tap_y // 2),
                        (0, 0),
                    ),
                )
                parity = (tap_z % 2, tap_x % 2, tap_y % 2)
                buckets[parity] = placed if parity not in buckets else buckets[parity] + placed
    planes_z = []
    for par_z in range(2):
        planes_x = []
        for par_x in range(2):
            planes_x.append(jnp.stack([buckets[par_z, par_x, par_y] for par_y in range(2)], axis=4))
        planes_z.append(jnp.stack(planes_x, axis=3))
    assembled = jnp.stack(planes_z, axis=2)
    assembled = assembled.reshape(
        leading, 2 * extent_z + 2, 2 * extent_x + 2, 2 * extent_y + 2, channels
    )
    return assembled[:, 1:-1, 1:-1, 1:-1, :]


def body(volume, targets, front_weight, stride_weight, hidden_weight, output_weight):
    highest = lax.Precision.HIGHEST
    slabs = lax.axis_size("slab")
    batches = lax.axis_size("batch")
    inner = front_weight.shape[-1]
    leading, thick, extent_x, extent_y, channels = volume.shape
    depth = thick * slabs
    outputs = output_weight.shape[-1]
    haloed = with_halo(volume, (("slab", 1),), 1)
    padded = jnp.pad(haloed, ((0, 0), (0, 0), (1, 1), (1, 1), (0, 0)))
    front_pre = conv_apply(padded, front_weight, thick, extent_x, extent_y, 1)
    front_act = jax.nn.silu(front_pre).astype(jnp.bfloat16)
    merged = front_act.reshape(leading, thick, extent_x, extent_y * inner)
    sample_act = lax.all_to_all(merged, "slab", split_axis=0, concat_axis=1, tiled=True)
    sample_act = sample_act.reshape(1, depth, extent_x, extent_y, inner)
    half_z = depth // 2
    half_x = extent_x // 2
    half_y = extent_y // 2
    cells = half_z * half_x * half_y
    stride_pad = jnp.pad(sample_act, ((0, 0), (1, 1), (1, 1), (1, 1), (0, 0)))
    partial_pre = conv_apply(stride_pad, stride_weight, half_z, half_x, half_y, 2)
    stride_pre = lax.psum_scatter(partial_pre, "chan", scatter_dimension=4, tiled=True)
    pooled = jnp.sum(jax.nn.silu(stride_pre), axis=(0, 1, 2, 3)) / cells
    hidden_pre = lax.psum(jnp.dot(pooled, hidden_weight, precision=highest), "chan")
    hidden_act = jax.nn.silu(hidden_pre)
    predicted = jnp.dot(hidden_act, output_weight, precision=highest)
    target_row = lax.dynamic_index_in_dim(targets, lax.axis_index("slab"), 0, keepdims=False)
    residual = predicted - target_row
    squared = jnp.sum(residual * residual)
    grad_output = jnp.outer(hidden_act, residual)
    grad_hidden_pre = jnp.dot(output_weight, residual, precision=highest) * swish_slope(hidden_pre)
    grad_hidden = jnp.outer(pooled, grad_hidden_pre)
    grad_pooled = jnp.dot(hidden_weight, grad_hidden_pre, precision=highest)
    grad_stride_pre = (grad_pooled / cells * swish_slope(stride_pre)).astype(jnp.bfloat16)
    full_grad = lax.all_gather(grad_stride_pre, "chan", axis=4, tiled=True)
    grad_stride = kernel_grad(stride_pad, full_grad, half_z, half_x, half_y, 2)
    grad_act = input_grad(full_grad, stride_weight, half_z, half_x, half_y).astype(jnp.bfloat16)
    returned = lax.all_to_all(
        grad_act.reshape(1, depth, extent_x, extent_y * inner),
        "slab",
        split_axis=1,
        concat_axis=0,
        tiled=True,
    )
    returned = returned.reshape(leading, thick, extent_x, extent_y, inner)
    grad_front_pre = (returned * swish_slope(front_pre)).astype(jnp.bfloat16)
    grad_front = kernel_grad(padded, grad_front_pre, thick, extent_x, extent_y, 1)
    grad_front, grad_stride, grad_hidden, grad_output, squared = lax.psum(
        (grad_front, grad_stride, grad_hidden, grad_output, squared), ("slab", "batch")
    )
    loss = (squared / (slabs * batches * outputs)).reshape(1)
    return (grad_front, grad_stride, grad_hidden, grad_output, loss)


def solution(mesh):
    in_specs = (
        P(("groups", "batch"), "slab", None, None, None),
        P(("groups", "batch"), None),
        P(None, None, None, None, "chan"),
        P(None, None, None, "chan", None),
        P("chan", None),
        P(),
    )
    out_specs = (
        P("groups", None, None, None, "chan"),
        P("groups", None, None, "chan", None),
        P(("groups", "chan"), None),
        P("groups", None),
        P("groups"),
    )
    return jax.shard_map(body, mesh=mesh, in_specs=in_specs, out_specs=out_specs, check_vma=False)
```

profile of v0, /device:TPU:0, one launch (start us, length us, event | category | flops | bytes accessed | tf_op | source)
XLA Modules:
  0.0 213.3 jit_solution(12655027647742667064)
XLA Ops:
  7.2 0.8 fusion.298
  8.0 4.9 %collective-permute-start = (bf16[4,1,4,8,128]{4,3,2,1,0:T(8,128)(2,1)S(1)}, bf16[4,1,4,8,128]{4,3,2,1,0:T(8,128)(2,1)S(1)}, u32[]{:S(2)}, u32[]{:S(2)}) collective-permute-start(bf16[4,1,4,8,128]{4,3,2,1,0:T(8,128)(2,1)S(1)} %get-tuple-element.63), channel_id=1, source_target_pairs={{0,4},{4,8},{8,12},{1,5},{5,9},{9,13},{2,6},{6,10},{10,14},{3,7},{... | collective-permute-start | bytes 98312 | tf_op jit(solution)/shard_map/ppermute | solution.py:15
  13.0 1.4 collective-permute-start.1
  14.5 4.4 %collective-permute-done.1 = bf16[4,1,4,8,128]{4,3,2,1,0:T(8,128)(2,1)S(1)} collective-permute-done((bf16[4,1,4,8,128]{4,3,2,1,0:T(8,128)(2,1)S(1)}, bf16[4,1,4,8,128]{4,3,2,1,0:T(8,128)(2,1)S(1)}, u32[]{:S(2)}, u32[]{:S(2)}) %collective-permute-start.1) | collective-permute-done | bytes 32800 | tf_op jit(solution)/shard_map/ppermute | solution.py:17
  18.9 1.0 select_maximum_fusion
  19.9 0.2 fusion.294
  20.2 0.6 copy-done.6
  25.4 9.3 %all_to_all.8 = bf16[4,2,4,512]{3,2,1,0:T(4,128)(2,1)S(1)} all-to-all(bf16[4,2,4,512]{3,2,1,0:T(4,128)(2,1)S(1)} %fusion.65), channel_id=1, replica_groups=mesh['groups'=2,'slab'=4,'batch'=2,'chan'=2] {'slab'}, dimensions={0} | all-to-all | bytes 65536 | tf_op jit(solution)/shard_map/all_to_all | solution.py:139
  35.1 0.2 fusion.296
  39.2 0.8 copy.165
  40.0 1.9 reshape.469
  41.9 6.1 %reduce-scatter.4.cloned.1.call-done = f32[128,32]{1,0:T(8,128)} async-done(((f32[256,32]{1,0:T(8,128)}), f32[128,32]{1,0:T(8,128)}) %reduce-scatter.4.cloned.1.call-update) | async-done | bytes 16400
  48.0 1.5 reshape.470
  49.5 0.4 copy.166
  50.1 2.5 %psum.42 = f32[128]{0:T(128)S(1)} all-reduce(f32[128]{0:T(128)S(1)} %convolution_bitcast_fusion.83), channel_id=1, replica_groups=mesh['groups'=2,'slab'=4,'batch'=2,'chan'=2] {'chan'}, use_global_device_ids=true, to_apply=%region_2.3 | all-reduce | flops 128 | bytes 1024 | tf_op jit(solution)/shard_map/psum | solution.py:149
  52.6 1.4 multiply_reduce_fusion.1
  54.4 1.8 all_gather.3
  65.4 0.7 reshape.468
  66.1 4.8 %all-to-all-start.1 = ((bf16[1,8,4,512]{3,2,0,1:T(4,128)(2,1)}), bf16[1,8,4,512]{3,2,0,1:T(4,128)(2,1)S(1)}, u32[]{:S(2)}, u32[]{:S(2)}) async-start(bf16[1,8,4,512]{3,2,0,1:T(4,128)(2,1)} %reshape.468), calls=%async_computation.1 | async-start | bytes 65536 | tf_op jit(solution)/shard_map/all_to_all | solution.py:163
  71.0 0.7 broadcast_multiply_fusion
  71.7 4.9 %all-to-all-done.1 = bf16[1,8,4,512]{3,2,0,1:T(4,128)(2,1)S(1)} async-done(((bf16[1,8,4,512]{3,2,0,1:T(4,128)(2,1)}), bf16[1,8,4,512]{3,2,0,1:T(4,128)(2,1)S(1)}, u32[]{:S(2)}, u32[]{:S(2)}) %all-to-all-start.1) | async-done | bytes 32800 | tf_op jit(solution)/shard_map/all_to_all | solution.py:163
  76.8 0.2 fusion.54
  77.0 0.2 fusion.53
  77.2 0.2 fusion.52
  77.4 0.2 fusion.51
  77.8 0.2 fusion.50
  78.0 0.2 fusion.49
  78.2 0.2 fusion.48
  78.5 0.2 fusion.47
  78.7 0.2 fusion.46
  78.9 0.2 fusion.45
  79.1 0.2 fusion.44
  79.3 0.2 fusion.43
  79.5 0.2 fusion.42
  79.7 0.2 fusion.41
  79.9 0.2 fusion.40
  80.5 0.2 fusion.37
  81.1 0.2 fusion.34
  81.5 0.2 fusion.33
  81.7 0.2 fusion.32
  81.9 0.2 fusion.31
  82.1 0.2 fusion.30
  82.4 0.9 copy-done.5
  83.4 20.3 %all-reduce.29 = (f32[128,4]{0,1:T(4,128)}, f32[]{:T(128)}) all-reduce(f32[128,4]{0,1:T(4,128)S(1)} %broadcast_multiply_fusion.1, f32[]{:T(128)} %get-tuple-element.65), channel_id=1, replica_groups=mesh['groups'=2,'slab'=4,'batch'=2,'chan'=2] {'slab','batch'}, use_global_device_ids=true, to_apply=%region_6.7 | all-reduce | flops 513 | bytes 4104 | tf_op jit(solution)/shard_map/psum | solution.py:173
  104.3 96.9 %all-reduce.33.cloned.1.call-done = (f32[3,3,3,128,64]{3,4,2,1,0:T(8,128)}, f32[3,3,3,64,256]{4,3,2,1,0:T(8,128)}, f32[128,128]{1,0:T(8,128)}) async-done(((f32[3,3,3,128,64]{3,4,2,1,0:T(8,128)}, f32[3,3,3,64,256]{4,3,2,1,0:T(8,128)}, f32[128,128]{1,0:T(8,128)}), (f32[3,3,3,128,64]{3,4,2,1,0:T(8,128)}, f32[3,3,3,64,256]{4,3,2,1,0:T(8,128)}, f32[128,128]{1,0:T(8,128)})) %all-reduce.33.cloned.1.call-update) | async-done | bytes 2719760 | tf_op jit(solution)/shard_map/psum | solution.py:173
  201.2 2.3 %copy.225 = f32[3,3,3,128,64]{3,4,2,1,0:T(8,128)} copy(f32[3,3,3,128,64]{3,4,2,1,0:T(8,128)} %get-tuple-element.73) | data formatting | bytes 1769472
  203.5 1.2 copy.226
  204.7 0.6 copy.227
  (204 shorter events, 19.8 us)
Async XLA Ops:
  7.2 42.8 %copy-start = (f32[128,128]{1,0:T(8,128)S(1)}, f32[128,128]{1,0:T(8,128)}, u32[]{:S(2)}) copy-start(f32[128,128]{1,0:T(8,128)} %param.10) | copy-start | bytes 196612
  7.2 40.8 %reduce-scatter.4.cloned.1.call-start = ((), (), s32[]{:S(2)}) async-start(), calls=%async_computation.3 | async-start | bytes 196608
  8.0 6.5 %collective-permute-start = (bf16[4,1,4,8,128]{4,3,2,1,0:T(8,128)(2,1)S(1)}, bf16[4,1,4,8,128]{4,3,2,1,0:T(8,128)(2,1)S(1)}, u32[]{:S(2)}, u32[]{:S(2)}) collective-permute-start(bf16[4,1,4,8,128]{4,3,2,1,0:T(8,128)(2,1)S(1)} %get-tuple-element.63), channel_id=1, source_target_pairs={{0,4},{4,8},{8,12},{1,5},{5,9},{9,13},{2,6},{6,10},{10,14},{3,7},{... | collective-permute-start | bytes 98312 | tf_op jit(solution)/shard_map/ppermute | solution.py:15
  12.9 7.2 %copy-start.4 = (bf16[4,2,4,8,128]{4,3,2,1,0:T(8,128)(2,1)S(1)}, bf16[4,2,4,8,128]{4,3,2,1,0:T(8,128)(2,1)}, u32[]{:S(2)}) copy-start(bf16[4,2,4,8,128]{4,3,2,1,0:T(8,128)(2,1)} %param.6) | copy-start | bytes 196612
  13.0 5.9 %collective-permute-start.1 = (bf16[4,1,4,8,128]{4,3,2,1,0:T(8,128)(2,1)S(1)}, bf16[4,1,4,8,128]{4,3,2,1,0:T(8,128)(2,1)S(1)}, u32[]{:S(2)}, u32[]{:S(2)}) collective-permute-start(bf16[4,1,4,8,128]{4,3,2,1,0:T(8,128)(2,1)S(1)} %get-tuple-element.64), channel_id=1, source_target_pairs={{4,0},{8,4},{12,8},{5,1},{9,5},{13,9},{6,2},{10,6},{14,10},{7,3},{... | collective-permute-start | bytes 98312 | tf_op jit(solution)/shard_map/ppermute | solution.py:17
  19.9 1.0 copy-start.6
  24.8 10.9 %copy-start.1 = (bf16[3,3,3,64,256]{4,3,2,1,0:T(8,128)(2,1)S(1)}, bf16[3,3,3,64,256]{4,3,2,1,0:T(8,128)(2,1)}, u32[]{:S(2)}) copy-start(bf16[3,3,3,64,256]{4,3,2,1,0:T(8,128)(2,1)} %param.9) | copy-start | bytes 2654212
  39.2 13.4 %copy-start.8 = (f32[128,4]{0,1:T(4,128)S(1)}, f32[128,4]{0,1:T(4,128)}, u32[]{:S(2)}) copy-start(f32[128,4]{0,1:T(4,128)} %param.11) | copy-start | bytes 6148
  64.7 12.0 %copy-start.2 = (f32[27,64,256]{2,1,0:T(8,128)}, f32[27,64,256]{2,1,0:T(8,128)S(1)}, u32[]{:S(2)}) copy-start(f32[27,64,256]{2,1,0:T(8,128)S(1)} %fusion) | copy-start | bytes 5308420
  66.1 10.5 %all-to-all-start.1 = ((bf16[1,8,4,512]{3,2,0,1:T(4,128)(2,1)}), bf16[1,8,4,512]{3,2,0,1:T(4,128)(2,1)S(1)}, u32[]{:S(2)}, u32[]{:S(2)}) async-start(bf16[1,8,4,512]{3,2,0,1:T(4,128)(2,1)} %reshape.468), calls=%async_computation.1 | async-start | bytes 65536 | tf_op jit(solution)/shard_map/all_to_all | solution.py:163
  71.0 130.2 %all-reduce.33.cloned.1.call-start = ((), (), s32[]{:S(2)}) async-start(), calls=%async_computation.4 | async-start | bytes 5439488 | tf_op jit(solution)/shard_map/psum | solution.py:173
  82.4 0.9 copy-start.5
  201.2 2.3 %copy-start.3 = (f32[3,3,3,64,256]{4,3,2,1,0:T(8,128)S(1)}, f32[3,3,3,64,256]{4,3,2,1,0:T(8,128)}, u32[]{:S(2)}) copy-start(f32[3,3,3,64,256]{4,3,2,1,0:T(8,128)} %get-tuple-element.74) | copy-start | bytes 5308420
  203.5 1.2 copy-start.7
Sparse Core Ops, SparseCore 0:
  42.0 5.8 reduce-scatter.3
  83.4 117.7 all-reduce.32
where the time goes:
time: 214 us; the launch traced here: 213 us
  waiting for transfers between devices  112 us (52%)
  blocking collectives  33.9 us (16%)
  matrix products  23.2 us (11%)
  between operations  16.7 us (8%)
  local copies, waits for them, and re-layouts  13.5 us (6%)
  starting transfers between devices  11.2 us (5%)
  other arithmetic  2.34 us (1%)
    psum x1, waiting for transfers between devices, body(): lax.psum((grad_front, grad_stride, grad_hidden, grad_output, squared), ('...  96.9 us
    psum x1, blocking collectives, body(): lax.psum((grad_front, grad_stride, grad_hidden, grad_output, squared), ('...  20.3 us
    unnamed x27, local copies, waits for them, and re-layouts  10.4 us
    dot_general x54, matrix products, kernel_grad(): lax.dot_general(flat_tap, flat_grad, (((0,), (0,)), ((), ())), preferred_...  10.2 us
    all_to_all x1, blocking collectives, body(): lax.all_to_all(merged, 'slab', split_axis=0, concat_axis=1, tiled=True)  9.32 us
    dot_general x54, matrix products, conv_apply(): jnp.dot(flat_tap, weight[tap_z, tap_x, tap_y], preferred_element_type=jnp...  7.54 us
    unnamed x3, waiting for transfers between devices  6.09 us
    all_to_all x1, waiting for transfers between devices, body(): lax.all_to_all(grad_act.reshape(1, depth, extent_x, extent_y * inner), 's...  4.94 us
  transfers between devices with their start and end apart: 5, of which 5 were waited for; matrix products, arithmetic and copies ran while one was open for 0% of the time, Pallas kernels for 0%

commit v1 on v0

--- a/solution.py
+++ b/solution.py
@@ -160,13 +160,19 @@
     full_grad = lax.all_gather(grad_stride_pre, "chan", axis=4, tiled=True)
     grad_stride = kernel_grad(stride_pad, full_grad, half_z, half_x, half_y, 2)
     grad_act = input_grad(full_grad, stride_weight, half_z, half_x, half_y).astype(jnp.bfloat16)
-    returned = lax.all_to_all(
-        grad_act.reshape(1, depth, extent_x, extent_y * inner),
-        "slab",
-        split_axis=1,
-        concat_axis=0,
-        tiled=True,
-    )
+
+    def divide_pairs_all(vals, named_axis):
+        return jnp.concatenate(
+            lax.all_to_all(
+                jnp.stack(jnp.split(vals, lax.axis_size(named_axis), 1)),
+                split_axis=0,
+                concat_axis=0,
+                axis_name=named_axis,
+            ),
+            0,
+        )
+
+    returned = divide_pairs_all(grad_act.reshape(1, depth, extent_x, extent_y * inner), "slab")
     returned = returned.reshape(leading, thick, extent_x, extent_y, inner)
     grad_front_pre = (returned * swish_slope(front_pre)).astype(jnp.bfloat16)
     grad_front = kernel_grad(padded, grad_front_pre, thick, extent_x, extent_y, 1)

time: 214 us -> 214 us (level)
  no operation moved by 1% of the time
where the time goes in v1:
time: 214 us; the launch traced here: 213 us
  waiting for transfers between devices  112 us (52%)
  blocking collectives  33.9 us (16%)
  matrix products  23.2 us (11%)
  between operations  16.7 us (8%)
  local copies, waits for them, and re-layouts  13 us (6%)
  starting transfers between devices  11.2 us (5%)
  other arithmetic  3.01 us (1%)
    psum x1, waiting for transfers between devices, body(): lax.psum((grad_front, grad_stride, grad_hidden, grad_output, squared), ('...  96.9 us
    psum x1, blocking collectives, body(): lax.psum((grad_front, grad_stride, grad_hidden, grad_output, squared), ('...  20.3 us
    unnamed x27, local copies, waits for them, and re-layouts  10.4 us
    dot_general x54, matrix products, kernel_grad(): lax.dot_general(flat_tap, flat_grad, (((0,), (0,)), ((), ())), preferred_...  10.2 us
    all_to_all x1, blocking collectives, body(): lax.all_to_all(merged, 'slab', split_axis=0, concat_axis=1, tiled=True)  9.32 us
    dot_general x54, matrix products, conv_apply(): jnp.dot(flat_tap, weight[tap_z, tap_x, tap_y], preferred_element_type=jnp...  7.54 us
    unnamed x3, waiting for transfers between devices  6.09 us
    all_to_all x1, waiting for transfers between devices, divide_pairs_all(): lax.all_to_all(jnp.stack(jnp.split(vals, lax.axis_size(named_axis), 1)),...  4.94 us
  transfers between devices with their start and end apart: 5, of which 5 were waited for; matrix products, arithmetic and copies ran while one was open for 0% of the time, Pallas kernels for 0%

profile of v1, /device:TPU:0, one launch (start us, length us, event | category | flops | bytes accessed | tf_op | source)
XLA Modules:
  0.0 213.4 jit_solution(3112192125102113100)
XLA Ops:
  7.2 0.8 fusion.299
  8.0 4.9 %collective-permute-start = (bf16[4,1,4,8,128]{4,3,2,1,0:T(8,128)(2,1)S(1)}, bf16[4,1,4,8,128]{4,3,2,1,0:T(8,128)(2,1)S(1)}, u32[]{:S(2)}, u32[]{:S(2)}) collective-permute-start(bf16[4,1,4,8,128]{4,3,2,1,0:T(8,128)(2,1)S(1)} %get-tuple-element.63), channel_id=1, source_target_pairs={{0,4},{4,8},{8,12},{1,5},{5,9},{9,13},{2,6},{6,10},{10,14},{3,7},{... | collective-permute-start | bytes 98312 | tf_op jit(solution)/shard_map/ppermute | solution.py:15
  13.0 1.4 collective-permute-start.1
  14.5 4.4 %collective-permute-done.1 = bf16[4,1,4,8,128]{4,3,2,1,0:T(8,128)(2,1)S(1)} collective-permute-done((bf16[4,1,4,8,128]{4,3,2,1,0:T(8,128)(2,1)S(1)}, bf16[4,1,4,8,128]{4,3,2,1,0:T(8,128)(2,1)S(1)}, u32[]{:S(2)}, u32[]{:S(2)}) %collective-permute-start.1) | collective-permute-done | bytes 32800 | tf_op jit(solution)/shard_map/ppermute | solution.py:17
  18.9 1.0 select_maximum_fusion
  19.9 0.2 fusion.295
  20.2 0.6 copy-done.6
  25.4 9.3 %all_to_all.14 = bf16[4,2,4,512]{3,2,1,0:T(4,128)(2,1)S(1)} all-to-all(bf16[4,2,4,512]{3,2,1,0:T(4,128)(2,1)S(1)} %fusion.66), channel_id=1, replica_groups=mesh['groups'=2,'slab'=4,'batch'=2,'chan'=2] {'slab'}, dimensions={0} | all-to-all | bytes 65536 | tf_op jit(solution)/shard_map/all_to_all | solution.py:139
  35.1 0.2 fusion.297
  39.2 0.8 copy.170
  40.0 1.9 reshape.463
  41.9 6.1 %reduce-scatter.4.cloned.1.call-done = f32[128,32]{1,0:T(8,128)} async-done(((f32[256,32]{1,0:T(8,128)}), f32[128,32]{1,0:T(8,128)}) %reduce-scatter.4.cloned.1.call-update) | async-done | bytes 16400
  48.0 1.5 reshape.464
  49.5 0.4 copy.171
  50.1 2.5 %psum.42 = f32[128]{0:T(128)S(1)} all-reduce(f32[128]{0:T(128)S(1)} %convolution_bitcast_fusion.83), channel_id=1, replica_groups=mesh['groups'=2,'slab'=4,'batch'=2,'chan'=2] {'chan'}, use_global_device_ids=true, to_apply=%region_2.3 | all-reduce | flops 128 | bytes 1024 | tf_op jit(solution)/shard_map/psum | solution.py:149
  52.6 1.4 multiply_reduce_fusion.1
  54.4 1.8 all_gather.3
  65.6 0.7 pad_maximum_fusion.1
  66.3 4.8 %all-to-all-start.1 = ((bf16[4,1,2,4,512]{4,2,3,1,0:T(2,128)(2,1)}), bf16[4,1,2,4,512]{4,2,3,1,0:T(2,128)(2,1)S(1)}, u32[]{:S(2)}, u32[]{:S(2)}) async-start(bf16[4,1,2,4,512]{4,2,3,1,0:T(2,128)(2,1)} %pad_maximum_fusion.1), calls=%async_computation.1 | async-start | bytes 65536 | tf_op jit(solution)/shard_map/all_to_all | solution.py:166
  71.1 0.7 broadcast_multiply_fusion
  71.8 4.9 %all-to-all-done.1 = bf16[4,1,2,4,512]{4,2,3,1,0:T(2,128)(2,1)S(1)} async-done(((bf16[4,1,2,4,512]{4,2,3,1,0:T(2,128)(2,1)}), bf16[4,1,2,4,512]{4,2,3,1,0:T(2,128)(2,1)S(1)}, u32[]{:S(2)}, u32[]{:S(2)}) %all-to-all-start.1) | async-done | bytes 32800 | tf_op jit(solution)/shard_map/all_to_all | solution.py:166
  76.9 0.2 fusion.54
  77.3 0.2 fusion.52
  77.5 0.2 fusion.51
  77.9 0.2 fusion.50
  78.1 0.2 fusion.49
  78.3 0.2 fusion.48
  78.6 0.2 fusion.47
  78.8 0.2 fusion.46
  79.0 0.2 fusion.45
  79.2 0.2 fusion.44
  79.4 0.2 fusion.43
  79.6 0.2 fusion.42
  79.8 0.2 fusion.41
  80.0 0.2 fusion.40
  80.6 0.2 fusion.37
  80.8 0.2 fusion.36
  81.2 0.2 fusion.34
  81.6 0.2 fusion.33
  81.8 0.2 fusion.32
  82.0 0.2 fusion.31
  82.2 0.2 fusion.30
  82.5 0.9 copy-done.5
  83.5 20.3 %all-reduce.29 = (f32[128,4]{0,1:T(4,128)}, f32[]{:T(128)}) all-reduce(f32[128,4]{0,1:T(4,128)S(1)} %broadcast_multiply_fusion.1, f32[]{:T(128)} %get-tuple-element.69), channel_id=1, replica_groups=mesh['groups'=2,'slab'=4,'batch'=2,'chan'=2] {'slab','batch'}, use_global_device_ids=true, to_apply=%region_6.7 | all-reduce | flops 513 | bytes 4104 | tf_op jit(solution)/shard_map/psum | solution.py:179
  104.4 96.9 %all-reduce.33.cloned.1.call-done = (f32[3,3,3,128,64]{3,4,2,1,0:T(8,128)}, f32[3,3,3,64,256]{4,3,2,1,0:T(8,128)}, f32[128,128]{1,0:T(8,128)}) async-done(((f32[3,3,3,128,64]{3,4,2,1,0:T(8,128)}, f32[3,3,3,64,256]{4,3,2,1,0:T(8,128)}, f32[128,128]{1,0:T(8,128)}), (f32[3,3,3,128,64]{3,4,2,1,0:T(8,128)}, f32[3,3,3,64,256]{4,3,2,1,0:T(8,128)}, f32[128,128]{1,0:T(8,128)})) %all-reduce.33.cloned.1.call-update) | async-done | bytes 2719760 | tf_op jit(solution)/shard_map/psum | solution.py:179
  201.3 2.3 %copy.232 = f32[3,3,3,128,64]{3,4,2,1,0:T(8,128)} copy(f32[3,3,3,128,64]{3,4,2,1,0:T(8,128)} %get-tuple-element.77) | data formatting | bytes 1769472
  203.6 1.2 copy.233
  204.8 0.6 copy.234
  (206 shorter events, 19.9 us)
Async XLA Ops:
  7.2 42.8 %copy-start = (f32[128,128]{1,0:T(8,128)S(1)}, f32[128,128]{1,0:T(8,128)}, u32[]{:S(2)}) copy-start(f32[128,128]{1,0:T(8,128)} %param.10) | copy-start | bytes 196612
  7.2 40.8 %reduce-scatter.4.cloned.1.call-start = ((), (), s32[]{:S(2)}) async-start(), calls=%async_computation.3 | async-start | bytes 196608
  8.0 6.5 %collective-permute-start = (bf16[4,1,4,8,128]{4,3,2,1,0:T(8,128)(2,1)S(1)}, bf16[4,1,4,8,128]{4,3,2,1,0:T(8,128)(2,1)S(1)}, u32[]{:S(2)}, u32[]{:S(2)}) collective-permute-start(bf16[4,1,4,8,128]{4,3,2,1,0:T(8,128)(2,1)S(1)} %get-tuple-element.63), channel_id=1, source_target_pairs={{0,4},{4,8},{8,12},{1,5},{5,9},{9,13},{2,6},{6,10},{10,14},{3,7},{... | collective-permute-start | bytes 98312 | tf_op jit(solution)/shard_map/ppermute | solution.py:15
  12.9 7.2 %copy-start.4 = (bf16[4,2,4,8,128]{4,3,2,1,0:T(8,128)(2,1)S(1)}, bf16[4,2,4,8,128]{4,3,2,1,0:T(8,128)(2,1)}, u32[]{:S(2)}) copy-start(bf16[4,2,4,8,128]{4,3,2,1,0:T(8,128)(2,1)} %param.6) | copy-start | bytes 196612
  13.0 5.9 %collective-permute-start.1 = (bf16[4,1,4,8,128]{4,3,2,1,0:T(8,128)(2,1)S(1)}, bf16[4,1,4,8,128]{4,3,2,1,0:T(8,128)(2,1)S(1)}, u32[]{:S(2)}, u32[]{:S(2)}) collective-permute-start(bf16[4,1,4,8,128]{4,3,2,1,0:T(8,128)(2,1)S(1)} %get-tuple-element.64), channel_id=1, source_target_pairs={{4,0},{8,4},{12,8},{5,1},{9,5},{13,9},{6,2},{10,6},{14,10},{7,3},{... | collective-permute-start | bytes 98312 | tf_op jit(solution)/shard_map/ppermute | solution.py:17
  19.9 1.0 copy-start.6
  24.8 10.9 %copy-start.1 = (bf16[3,3,3,64,256]{4,3,2,1,0:T(8,128)(2,1)S(1)}, bf16[3,3,3,64,256]{4,3,2,1,0:T(8,128)(2,1)}, u32[]{:S(2)}) copy-start(bf16[3,3,3,64,256]{4,3,2,1,0:T(8,128)(2,1)} %param.9) | copy-start | bytes 2654212
  39.2 13.4 %copy-start.8 = (f32[128,4]{0,1:T(4,128)S(1)}, f32[128,4]{0,1:T(4,128)}, u32[]{:S(2)}) copy-start(f32[128,4]{0,1:T(4,128)} %param.11) | copy-start | bytes 6148
  64.7 7.1 %copy-start.2 = (f32[27,64,256]{2,1,0:T(8,128)}, f32[27,64,256]{2,1,0:T(8,128)S(1)}, u32[]{:S(2)}) copy-start(f32[27,64,256]{2,1,0:T(8,128)S(1)} %fusion) | copy-start | bytes 5308420
  66.3 10.5 %all-to-all-start.1 = ((bf16[4,1,2,4,512]{4,2,3,1,0:T(2,128)(2,1)}), bf16[4,1,2,4,512]{4,2,3,1,0:T(2,128)(2,1)S(1)}, u32[]{:S(2)}, u32[]{:S(2)}) async-start(bf16[4,1,2,4,512]{4,2,3,1,0:T(2,128)(2,1)} %pad_maximum_fusion.1), calls=%async_computation.1 | async-start | bytes 65536 | tf_op jit(solution)/shard_map/all_to_all | solution.py:166
  71.1 130.2 %all-reduce.33.cloned.1.call-start = ((), (), s32[]{:S(2)}) async-start(), calls=%async_computation.4 | async-start | bytes 5439488 | tf_op jit(solution)/shard_map/psum | solution.py:179
  82.4 0.9 copy-start.5
  201.3 2.3 %copy-start.3 = (f32[3,3,3,64,256]{4,3,2,1,0:T(8,128)S(1)}, f32[3,3,3,64,256]{4,3,2,1,0:T(8,128)}, u32[]{:S(2)}) copy-start(f32[3,3,3,64,256]{4,3,2,1,0:T(8,128)} %get-tuple-element.78) | copy-start | bytes 5308420
  203.6 1.2 copy-start.7
Sparse Core Ops, SparseCore 0:
  42.0 5.8 reduce-scatter.3
  83.5 117.7 all-reduce.32
